TPU v7x, 32 devices: a whole 2x2x4 slice. The times are simulated.
32 devices in a mesh: expert: 4 (over y, x), shard: 8 (over z, core).
Axes of the slice: x: 2, y: 2, z: 4, core: 2. Of those that a mesh axis runs over, the one named last changes fastest.
Arguments:
- hidden: bfloat16 [64, 4096], P('shard'), may hold values from -6 to 6
- queries: bfloat16 [64, 32, 128], P('shard', 'expert'), may hold values from -30 to 30
- key_cache: bfloat16 [64, 512, 8, 128], P('shard', None, 'expert'), may hold values from -16 to 16
- value_cache: bfloat16 [64, 512, 8, 128], P('shard', None, 'expert'), may hold values from -6 to 6
- out_weight: bfloat16 [4096, 4096], P('expert', 'shard'), may hold values from -0.09375 to 0.09375
- norm_gain: bfloat16 [4096], replicated, may hold values from 0.099609375 to 1.8984375
- router: bfloat16 [4096, 8], replicated, may hold values from -0.09375 to 0.09375
- expert_ids: int32 [64, 2], replicated, may hold values from 0 to 7, all different within a row; in each aligned block of 64 rows (0 to 63, 64 to 127, ...) at most 32 rows name the same one
- gate_weight: bfloat16 [8, 4096, 14336], P('expert', None, 'shard'), may hold values from -0.09375 to 0.09375
- up_weight: bfloat16 [8, 4096, 14336], P('expert', None, 'shard'), may hold values from -0.09375 to 0.09375
- down_weight: bfloat16 [8, 14336, 4096], P('expert', 'shard'), may hold values from -0.046875 to 0.046875
Outputs:
- layer_out: bfloat16 [64, 4096], P('shard')
Inputs may be any that keep to these rules, and one draw needn't show every extreme that they name: `expert_ids`: each token names two different experts; over all 64 tokens no expert is named by more than 32 tokens, a bound that some block reaches.
All inputs are finite; a program needn't handle non-finite values.
Results may differ from a plain program's by a relative error of at most 0.008.
Values may be sent and summed in bfloat16 or wider, within the bound.
A program may use at most 128 MiB of HBM per device.

v0:
```python
import math
import jax
import jax.numpy as jnp
from jax import lax
from jax.sharding import PartitionSpec as P


def on_device(
    hidden,
    queries,
    key_cache,
    value_cache,
    out_weight,
    norm_gain,
    router,
    expert_ids,
    gate_weight,
    up_weight,
    down_weight,
):
    count_local, heads_local, head_size = queries.shape
    kv_local = key_cache.shape[2]
    per_kv = heads_local // kv_local
    query_blocks = queries.reshape(count_local, kv_local, per_kv, head_size)
    scores = jnp.einsum(
        "tkgd,tpkd->tkgp", query_blocks, key_cache, preferred_element_type=jnp.float32
    ) / math.sqrt(head_size)
    attn_weights = jax.nn.softmax(scores, axis=-1).astype(jnp.bfloat16)
    attended = jnp.einsum(
        "tkgp,tpkd->tkgd", attn_weights, value_cache, preferred_element_type=jnp.float32
    )
    attended = attended.astype(jnp.bfloat16).reshape(count_local, heads_local * head_size)
    all_attended = lax.all_gather(attended, "shard", axis=0, tiled=True)
    partial_cols = jnp.dot(all_attended, out_weight, preferred_element_type=jnp.float32)
    partial_heads = lax.all_to_all(partial_cols, "shard", split_axis=0, concat_axis=1, tiled=True)
    attn_out = lax.psum(partial_heads, "expert")
    stream = hidden.astype(jnp.float32) + attn_out
    scaled = stream * lax.rsqrt(jnp.mean(stream * stream, axis=-1, keepdims=True) + 1e-05)
    normed = (scaled * norm_gain.astype(jnp.float32)).astype(jnp.bfloat16)
    everyone = lax.all_gather(normed, "shard", axis=0, tiled=True)
    token_count = everyone.shape[0]
    logits = jnp.dot(everyone, router, preferred_element_type=jnp.float32)
    top_first = jnp.take_along_axis(logits, expert_ids[:, 0:1], axis=1)[:, 0]
    top_second = jnp.take_along_axis(logits, expert_ids[:, 1:2], axis=1)[:, 0]
    weight_first = 1.0 / (1.0 + jnp.exp(top_second - top_first))
    weight_second = 1.0 / (1.0 + jnp.exp(top_first - top_second))
    local_experts = gate_weight.shape[0]
    group_index = lax.axis_index("expert")
    summed = jnp.zeros((token_count, everyone.shape[1]), jnp.float32)
    for member in range(local_experts):
        expert = group_index * local_experts + member
        in_first = expert_ids[:, 0] == expert
        in_second = expert_ids[:, 1] == expert
        routed_weight = jnp.where(in_first, weight_first, 0.0) + jnp.where(
            in_second, weight_second, 0.0
        )
        gated = jnp.dot(everyone, gate_weight[member], preferred_element_type=jnp.float32)
        upward = jnp.dot(everyone, up_weight[member], preferred_element_type=jnp.float32)
        activated = (jax.nn.silu(gated) * upward).astype(jnp.bfloat16)
        expert_out = jnp.dot(activated, down_weight[member], preferred_element_type=jnp.float32)
        summed = summed + routed_weight[:, None] * expert_out
    reduced = lax.psum_scatter(summed, "shard", scatter_dimension=0, tiled=True)
    expert_mix = lax.psum(reduced, "expert")
    return (stream + expert_mix).astype(jnp.bfloat16)


def solution(mesh):
    in_specs = (
        P("shard", None),
        P("shard", "expert", None),
        P("shard", None, "expert", None),
        P("shard", None, "expert", None),
        P("expert", "shard"),
        P(),
        P(),
        P(),
        P("expert", None, "shard"),
        P("expert", None, "shard"),
        P("expert", "shard", None),
    )
    out_specs = P("shard", None)
    return jax.shard_map(
        on_device, mesh=mesh, in_specs=in_specs, out_specs=out_specs, check_vma=False
    )
```

profile of v0, /device:TPU:0, one launch (start us, length us, event | category | flops | bytes accessed | tf_op | source)
XLA Modules:
  0.0 225.8 jit_solution(6295233523832174419)
XLA Ops:
  6.5 1.6 copy-done
  8.1 1.4 fusion.46
  9.7 2.0 fusion.49
  11.8 15.7 %all_gather.6 = bf16[64,1024]{1,0:T(8,128)(2,1)S(1)} all-gather(bf16[8,1024]{1,0:T(8,128)(2,1)S(1)} %reshape.37), channel_id=1, replica_groups=mesh['expert'=4,'shard'=8] {'shard'}, dimensions={0}, use_global_device_ids=true | all-gather | bytes 147456 | tf_op jit(solution)/shard_map/all_gather | solution.py:33
  27.5 2.2 convolution_bitcast_fusion
  29.7 4.6 %all-to-all-start = ((f32[8,8,512]{2,1,0:T(8,128)}), f32[8,8,512]{2,1,0:T(8,128)S(1)}, u32[]{:S(2)}, u32[]{:S(2)}) async-start(f32[8,8,512]{2,1,0:T(8,128)} %convolution_bitcast_fusion), calls=%async_computation | async-start | bytes 262144 | tf_op jit(solution)/shard_map/all_to_all | solution.py:35
  34.3 0.7 convert_element_type.27
  35.0 0.8 fusion.78
  35.8 5.2 %all-to-all-done = f32[8,8,512]{2,1,0:T(8,128)S(1)} async-done(((f32[8,8,512]{2,1,0:T(8,128)}), f32[8,8,512]{2,1,0:T(8,128)S(1)}, u32[]{:S(2)}, u32[]{:S(2)}) %all-to-all-start) | async-done | bytes 131104 | tf_op jit(solution)/shard_map/all_to_all | solution.py:35
  41.0 0.6 copy-done.4
  41.8 41.4 %all-reduce.3.cloned.1.call-done = f32[8,4096]{1,0:T(8,128)} async-done(((f32[8,4096]{1,0:T(8,128)}), f32[8,4096]{1,0:T(8,128)}) %all-reduce.3.cloned.1.call-update) | async-done | bytes 131088 | tf_op jit(solution)/shard_map/psum | solution.py:36
  83.2 1.1 multiply_reduce_fusion
  84.2 1.0 multiply_convert_fusion
  85.2 14.7 %all_gather.7 = bf16[64,4096]{1,0:T(8,128)(2,1)S(1)} all-gather(bf16[8,4096]{1,0:T(8,128)(2,1)S(1)} %multiply_convert_fusion), channel_id=1, replica_groups=mesh['expert'=4,'shard'=8] {'shard'}, dimensions={0}, use_global_device_ids=true | all-gather | bytes 589824 | tf_op jit(solution)/shard_map/all_gather | solution.py:40
  100.0 6.5 %fusion.5 = f32[64,1792]{1,0:T(8,128)S(1)} fusion(bf16[64,4096]{1,0:T(8,128)(2,1)S(1)} %all_gather.7, bf16[2,4096,1792]{2,1,0:T(8,128)(2,1)} %param.21), kind=kOutput, calls=%fused_computation.7 | convolution fusion | flops 939524096 | bytes 15663104 | tf_op jit(solution)/shard_map/dot_general | solution.py:57
  106.4 6.4 %fusion.11 = f32[64,1792]{1,0:T(8,128)S(1)} fusion(bf16[64,4096]{1,0:T(8,128)(2,1)S(1)} %all_gather.7, bf16[2,4096,1792]{2,1,0:T(8,128)(2,1)} %param.21), kind=kOutput, calls=%fused_computation.13 | convolution fusion | flops 939524096 | bytes 15663104 | tf_op jit(solution)/shard_map/dot_general | solution.py:57
  112.9 0.2 fusion.80
  113.2 0.7 gather_fusion
  113.9 0.7 gather_fusion.1
  114.7 13.1 %fusion.25 = f32[64,4096]{1,0:T(8,128)} fusion(bf16[2,1792,4096]{2,1,0:T(8,128)(2,1)} %param.23, bf16[64,4096]{1,0:T(8,128)(2,1)S(1)} %all_gather.7, bf16[2,4096,1792]{2,1,0:T(8,128)(2,1)} %param.22, f32[64]{0:T(128)S(1)} %fusion.73, f32[64,1792]{1,0:T(8,128)S(1)} %fusion.5), kind=kOutput, calls=%fused_computation.23 | convolution fusion | flops 1879998464 | bytes 31392000 | tf_op jit(solution)/shard_map/dot_general | solution.py:60
  127.8 13.6 %fusion.22 = f32[64,4096]{1,0:T(8,128)} fusion(f32[64,4096]{1,0:T(8,128)} %fusion.25, bf16[2,1792,4096]{2,1,0:T(8,128)(2,1)} %param.23, bf16[64,4096]{1,0:T(8,128)(2,1)S(1)} %all_gather.7, bf16[2,4096,1792]{2,1,0:T(8,128)(2,1)} %param.22, f32[64]{0:T(128)S(1)} %get-tuple-element.6, f32[64,1792]{1,0:T(8,128)S(1)} %fusion.11), kind=kOutput, calls=%fused_computation.22 | convolution fusion | flops 1880260608 | bytes 32440576 | tf_op jit(solution)/shard_map/dot_general | solution.py:60
  141.5 32.9 %reduce-scatter.2.cloned.1.call-done = f32[8,4096]{1,0:T(8,128)} async-done(((f32[64,4096]{1,0:T(8,128)}), f32[8,4096]{1,0:T(8,128)}) %reduce-scatter.2.cloned.1.call-update) | async-done | bytes 131088 | tf_op jit(solution)/shard_map/reduce_scatter | solution.py:62
  174.4 43.3 %all-reduce.5.cloned.1.call-done = f32[8,4096]{1,0:T(8,128)} async-done(((f32[8,4096]{1,0:T(8,128)}), f32[8,4096]{1,0:T(8,128)}) %all-reduce.5.cloned.1.call-update) | async-done | bytes 131088 | tf_op jit(solution)/shard_map/psum | solution.py:63
  217.7 1.6 add_convert_fusion
  (27 shorter events, 0.5 us)
Async XLA Ops:
  6.5 1.6 copy-start
  29.7 11.3 %all-to-all-start = ((f32[8,8,512]{2,1,0:T(8,128)}), f32[8,8,512]{2,1,0:T(8,128)S(1)}, u32[]{:S(2)}, u32[]{:S(2)}) async-start(f32[8,8,512]{2,1,0:T(8,128)} %convolution_bitcast_fusion), calls=%async_computation | async-start | bytes 262144 | tf_op jit(solution)/shard_map/all_to_all | solution.py:35
  34.3 48.9 %all-reduce.3.cloned.1.call-start = ((), (), s32[]{:S(2)}) async-start(), calls=%async_computation.2 | async-start | bytes 262144 | tf_op jit(solution)/shard_map/psum | solution.py:36
  41.0 0.6 copy-start.4
  41.7 132.7 %reduce-scatter.2.cloned.1.call-start = ((), (), s32[]{:S(2)}) async-start(), calls=%async_computation.3 | async-start | bytes 1179648 | tf_op jit(solution)/shard_map/reduce_scatter | solution.py:62
  100.0 12.9 %copy-start.5 = (bf16[4096,8]{0,1:T(8,128)(2,1)S(1)}, bf16[4096,8]{0,1:T(8,128)(2,1)}, u32[]{:S(2)}) copy-start(bf16[4096,8]{0,1:T(8,128)(2,1)} %param.19) | copy-start | bytes 196612
  100.0 14.7 %copy-start.6 = (s32[64,2]{0,1:T(2,128)S(1)}, s32[64,2]{0,1:T(2,128)}, u32[]{:S(2)}) copy-start(s32[64,2]{0,1:T(2,128)} %param.20) | copy-start | bytes 1540
  127.8 91.4 %copy-start.1 = (bf16[8,512,2,128]{3,2,1,0:T(2,128)(2,1)S(1)}, bf16[8,512,2,128]{3,2,1,0:T(2,128)(2,1)}, u32[]{:S(2)}) copy-start(bf16[8,512,2,128]{3,2,1,0:T(2,128)(2,1)} %param.15) | copy-start | bytes 6291460
  127.8 89.9 %copy-start.2 = (f32[8,4096]{1,0:T(8,128)S(1)}, f32[8,4096]{1,0:T(8,128)}, u32[]{:S(2)}) copy-start(f32[8,4096]{1,0:T(8,128)} %all-reduce.3.cloned.1.call-done) | copy-start | bytes 393220
  127.8 89.9 %copy-start.3 = (bf16[8,4096]{1,0:T(8,128)(2,1)S(1)}, bf16[8,4096]{1,0:T(8,128)(2,1)}, u32[]{:S(2)}) copy-start(bf16[8,4096]{1,0:T(8,128)(2,1)} %param.13) | copy-start | bytes 196612
  141.5 76.2 %all-reduce.5.cloned.1.call-start = ((), (), s32[]{:S(2)}) async-start(), calls=%async_computation.4 | async-start | bytes 262144 | tf_op jit(solution)/shard_map/psum | solution.py:63
Sparse Core Ops, SparseCore 0:
  41.8 41.2 all-reduce.2
  141.6 32.7 reduce-scatter.1
  177.3 40.3 all-reduce.4
where the time goes:
time: 226 us
  waiting for transfers between devices  123 us (54%)
  matrix products  45.5 us (20%)
  blocking collectives  30.5 us (13%)
  between operations  13.2 us (6%)
  other arithmetic  5.35 us (2%)
  starting transfers between devices  4.72 us (2%)
  local copies, waits for them, and re-layouts  3.76 us (2%)
    psum x1, waiting for transfers between devices, on_device(): expert_mix = lax.psum(reduced, 'expert')  43.3 us
    psum x1, waiting for transfers between devices, on_device(): attn_out = lax.psum(partial_heads, 'expert')  41.4 us
    reduce_scatter x1, waiting for transfers between devices, on_device(): reduced = lax.psum_scatter(summed, 'shard', scatter_dimension=0, tiled=True)  32.9 us
    dot_general x2, matrix products, on_device(): jnp.dot(activated, down_weight[member], preferred_element_type=jnp.float32)  26.7 us
    all_gather x1, blocking collectives, on_device(): all_attended = lax.all_gather(attended, 'shard', axis=0, tiled=True)  15.7 us
    all_gather x1, blocking collectives, on_device(): everyone = lax.all_gather(normed, 'shard', axis=0, tiled=True)  14.7 us
    dot_general x2, matrix products, on_device(): jnp.dot(everyone, gate_weight[member], preferred_element_type=jnp.float32)  12.9 us
    all_to_all x1, waiting for transfers between devices, on_device(): lax.all_to_all(partial_cols, 'shard', split_axis=0, concat_axis=1, tiled=...  5.22 us
  transfers between devices with their start and end apart: 4, of which 4 were waited for; matrix products, arithmetic and copies ran while one was open for 1% of the time, Pallas kernels for 0%

commit v1 on v0

--- a/solution.py
+++ b/solution.py
@@ -60,7 +60,7 @@
         expert_out = jnp.dot(activated, down_weight[member], preferred_element_type=jnp.float32)
         summed = summed + routed_weight[:, None] * expert_out
     reduced = lax.psum_scatter(summed, "shard", scatter_dimension=0, tiled=True)
-    expert_mix = lax.psum(reduced, "expert")
+    expert_mix = jax.lax.all_gather(reduced, "expert").sum(axis=0)
     return (stream + expert_mix).astype(jnp.bfloat16)
 
 

time: 226 us -> 193 us (0.85)
  waiting for transfers between devices: 123 us -> 79.5 us
  blocking collectives: 30.5 us -> 40.8 us
    psum x1 -> x0, waiting for transfers between devices: 43.3 us -> none  [on_device(): expert_mix = lax.psum(reduced, 'expert')]
    all_gather x0 -> x1, blocking collectives: none -> 10.3 us  [on_device(): expert_mix = jax.lax.all_gather(reduced, 'expert').sum(axis=0)]
  transfers between devices with their start and end apart: 4 -> 3, of which waited for: 4 -> 3; matrix products, arithmetic and copies ran while one was open for 1% -> 1% of each run, Pallas kernels for 0% -> 0%
where the time goes in v1:
time: 193 us; the launch traced here: 192 us
  waiting for transfers between devices  79.5 us (41%)
  matrix products  45.5 us (24%)
  blocking collectives  40.8 us (21%)
  between operations  13.5 us (7%)
  starting transfers between devices  4.68 us (2%)
  other arithmetic  4.48 us (2%)
  local copies, waits for them, and re-layouts  3.75 us (2%)
    psum x1, waiting for transfers between devices, on_device(): attn_out = lax.psum(partial_heads, 'expert')  41.4 us
    reduce_scatter x1, waiting for transfers between devices, on_device(): reduced = lax.psum_scatter(summed, 'shard', scatter_dimension=0, tiled=True)  32.9 us
    dot_general x2, matrix products, on_device(): jnp.dot(activated, down_weight[member], preferred_element_type=jnp.float32)  26.8 us
    all_gather x1, blocking collectives, on_device(): all_attended = lax.all_gather(attended, 'shard', axis=0, tiled=True)  15.7 us
    all_gather x1, blocking collectives, on_device(): everyone = lax.all_gather(normed, 'shard', axis=0, tiled=True)  14.7 us
    dot_general x2, matrix products, on_device(): jnp.dot(everyone, gate_weight[member], preferred_element_type=jnp.float32)  12.9 us
    all_gather x1, blocking collectives, on_device(): expert_mix = jax.lax.all_gather(reduced, 'expert').sum(axis=0)  10.3 us
    all_to_all x1, waiting for transfers between devices, on_device(): lax.all_to_all(partial_cols, 'shard', split_axis=0, concat_axis=1, tiled=...  5.22 us
  transfers between devices with their start and end apart: 3, of which 3 were waited for; matrix products, arithmetic and copies ran while one was open for 1% of the time, Pallas kernels for 0%

profile of v1, /device:TPU:0, one launch (start us, length us, event | category | flops | bytes accessed | tf_op | source)
XLA Modules:
  0.0 192.3 jit_solution(8444110503343114586)
XLA Ops:
  6.5 1.6 copy-done
  8.1 1.4 fusion.46
  9.7 2.0 %fusion.49 = bf16[8,2,4,128]{3,2,1,0:T(4,128)(2,1)S(1)} fusion(bf16[8,512,2,128]{3,2,1,0:T(2,128)(2,1)} %param.16, f32[8,2,4]{2,1,0:T(2,128)S(1)} %fusion.79, f32[8,2,4,512]{3,2,1,0:T(4,128)S(1)} %fusion.46), kind=kOutput, calls=%fused_computation.36 | convolution fusion | flops 8495679 | bytes 2244864 | tf_op jit(solution)/shard_map/tkgp,tpkd->tkgd/dot_general | solution.py:29
  11.8 15.7 %all_gather.12 = bf16[64,1024]{1,0:T(8,128)(2,1)S(1)} all-gather(bf16[8,1024]{1,0:T(8,128)(2,1)S(1)} %reshape.37), channel_id=1, replica_groups=mesh['expert'=4,'shard'=8] {'shard'}, dimensions={0}, use_global_device_ids=true | all-gather | bytes 147456 | tf_op jit(solution)/shard_map/all_gather | solution.py:33
  27.5 2.2 %convolution_bitcast_fusion = f32[8,8,512]{2,1,0:T(8,128)} fusion(bf16[64,1024]{1,0:T(8,128)(2,1)S(1)} %all_gather.12, bf16[1024,512]{1,0:T(8,128)(2,1)} %param.17), kind=kOutput, calls=%fused_computation.34 | convolution fusion | flops 67108864 | bytes 1310720 | tf_op jit(solution)/shard_map/dot_general | solution.py:34
  29.7 4.6 %all-to-all-start = ((f32[8,8,512]{2,1,0:T(8,128)}), f32[8,8,512]{2,1,0:T(8,128)S(1)}, u32[]{:S(2)}, u32[]{:S(2)}) async-start(f32[8,8,512]{2,1,0:T(8,128)} %convolution_bitcast_fusion), calls=%async_computation | async-start | bytes 262144 | tf_op jit(solution)/shard_map/all_to_all | solution.py:35
  34.3 0.7 convert_element_type.27
  35.0 0.8 fusion.78
  35.8 5.2 %all-to-all-done = f32[8,8,512]{2,1,0:T(8,128)S(1)} async-done(((f32[8,8,512]{2,1,0:T(8,128)}), f32[8,8,512]{2,1,0:T(8,128)S(1)}, u32[]{:S(2)}, u32[]{:S(2)}) %all-to-all-start) | async-done | bytes 131104 | tf_op jit(solution)/shard_map/all_to_all | solution.py:35
  41.0 0.6 copy-done.4
  41.8 41.4 %all-reduce.2.cloned.1.call-done = f32[8,4096]{1,0:T(8,128)} async-done(((f32[8,4096]{1,0:T(8,128)}), f32[8,4096]{1,0:T(8,128)}) %all-reduce.2.cloned.1.call-update) | async-done | bytes 131088 | tf_op jit(solution)/shard_map/psum | solution.py:36
  83.2 1.1 multiply_reduce_fusion
  84.2 1.0 multiply_convert_fusion
  85.2 14.7 %all_gather.13 = bf16[64,4096]{1,0:T(8,128)(2,1)S(1)} all-gather(bf16[8,4096]{1,0:T(8,128)(2,1)S(1)} %multiply_convert_fusion), channel_id=1, replica_groups=mesh['expert'=4,'shard'=8] {'shard'}, dimensions={0}, use_global_device_ids=true | all-gather | bytes 589824 | tf_op jit(solution)/shard_map/all_gather | solution.py:40
  100.0 6.5 %fusion.5 = f32[64,1792]{1,0:T(8,128)S(1)} fusion(bf16[64,4096]{1,0:T(8,128)(2,1)S(1)} %all_gather.13, bf16[2,4096,1792]{2,1,0:T(8,128)(2,1)} %param.21), kind=kOutput, calls=%fused_computation.7 | convolution fusion | flops 939524096 | bytes 15663104 | tf_op jit(solution)/shard_map/dot_general | solution.py:57
  106.4 6.4 %fusion.11 = f32[64,1792]{1,0:T(8,128)S(1)} fusion(bf16[64,4096]{1,0:T(8,128)(2,1)S(1)} %all_gather.13, bf16[2,4096,1792]{2,1,0:T(8,128)(2,1)} %param.21), kind=kOutput, calls=%fused_computation.13 | convolution fusion | flops 939524096 | bytes 15663104 | tf_op jit(solution)/shard_map/dot_general | solution.py:57
  112.9 0.2 fusion.80
  113.1 0.7 gather_fusion
  113.9 0.7 gather_fusion.1
  114.7 13.1 %fusion.25 = f32[64,4096]{1,0:T(8,128)} fusion(bf16[2,1792,4096]{2,1,0:T(8,128)(2,1)} %param.23, bf16[64,4096]{1,0:T(8,128)(2,1)S(1)} %all_gather.13, bf16[2,4096,1792]{2,1,0:T(8,128)(2,1)} %param.22, f32[64]{0:T(128)S(1)} %fusion.73, f32[64,1792]{1,0:T(8,128)S(1)} %fusion.5), kind=kOutput, calls=%fused_computation.23 | convolution fusion | flops 1879998464 | bytes 31392000 | tf_op jit(solution)/shard_map/dot_general | solution.py:60
  127.8 13.6 %fusion.22 = f32[64,4096]{1,0:T(8,128)} fusion(f32[64,4096]{1,0:T(8,128)} %fusion.25, bf16[2,1792,4096]{2,1,0:T(8,128)(2,1)} %param.23, bf16[64,4096]{1,0:T(8,128)(2,1)S(1)} %all_gather.13, bf16[2,4096,1792]{2,1,0:T(8,128)(2,1)} %param.22, f32[64]{0:T(128)S(1)} %get-tuple-element.6, f32[64,1792]{1,0:T(8,128)S(1)} %fusion.11), kind=kOutput, calls=%fused_computation.22 | convolution fusion | flops 1880260608 | bytes 32440576 | tf_op jit(solution)/shard_map/dot_general | solution.py:60
  141.5 32.9 %reduce-scatter.2.cloned.1.call-done = f32[8,4096]{1,0:T(8,128)} async-done(((f32[64,4096]{1,0:T(8,128)}), f32[8,4096]{1,0:T(8,128)}) %reduce-scatter.2.cloned.1.call-update) | async-done | bytes 131088 | tf_op jit(solution)/shard_map/reduce_scatter | solution.py:62
  174.4 10.3 %all-gather = f32[32,4096]{1,0:T(8,128)S(1)} all-gather(f32[8,4096]{1,0:T(8,128)} %reduce-scatter.2.cloned.1.call-done), channel_id=2, replica_groups=mesh['expert'=4,'shard'=8] {'expert'}, dimensions={0}, use_global_device_ids=true | all-gather | bytes 655360 | tf_op jit(solution)/shard_map/all_gather | solution.py:63
  184.8 0.7 add_convert_fusion
  (26 shorter events, 0.5 us)
Async XLA Ops:
  6.5 1.6 copy-start
  29.7 11.3 %all-to-all-start = ((f32[8,8,512]{2,1,0:T(8,128)}), f32[8,8,512]{2,1,0:T(8,128)S(1)}, u32[]{:S(2)}, u32[]{:S(2)}) async-start(f32[8,8,512]{2,1,0:T(8,128)} %convolution_bitcast_fusion), calls=%async_computation | async-start | bytes 262144 | tf_op jit(solution)/shard_map/all_to_all | solution.py:35
  34.3 48.9 %all-reduce.2.cloned.1.call-start = ((), (), s32[]{:S(2)}) async-start(), calls=%async_computation.2 | async-start | bytes 262144 | tf_op jit(solution)/shard_map/psum | solution.py:36
  41.0 0.6 copy-start.4
  41.7 132.7 %reduce-scatter.2.cloned.1.call-start = ((), (), s32[]{:S(2)}) async-start(), calls=%async_computation.3 | async-start | bytes 1179648 | tf_op jit(solution)/shard_map/reduce_scatter | solution.py:62
  100.0 12.9 %copy-start.5 = (bf16[4096,8]{0,1:T(8,128)(2,1)S(1)}, bf16[4096,8]{0,1:T(8,128)(2,1)}, u32[]{:S(2)}) copy-start(bf16[4096,8]{0,1:T(8,128)(2,1)} %param.19) | copy-start | bytes 196612
  100.0 14.7 %copy-start.6 = (s32[64,2]{0,1:T(2,128)S(1)}, s32[64,2]{0,1:T(2,128)}, u32[]{:S(2)}) copy-start(s32[64,2]{0,1:T(2,128)} %param.20) | copy-start | bytes 1540
  127.8 57.6 %copy-start.1 = (bf16[8,512,2,128]{3,2,1,0:T(2,128)(2,1)S(1)}, bf16[8,512,2,128]{3,2,1,0:T(2,128)(2,1)}, u32[]{:S(2)}) copy-start(bf16[8,512,2,128]{3,2,1,0:T(2,128)(2,1)} %param.15) | copy-start | bytes 6291460
  127.8 56.9 %copy-start.2 = (f32[8,4096]{1,0:T(8,128)S(1)}, f32[8,4096]{1,0:T(8,128)}, u32[]{:S(2)}) copy-start(f32[8,4096]{1,0:T(8,128)} %all-reduce.2.cloned.1.call-done) | copy-start | bytes 393220
  127.8 56.9 %copy-start.3 = (bf16[8,4096]{1,0:T(8,128)(2,1)S(1)}, bf16[8,4096]{1,0:T(8,128)(2,1)}, u32[]{:S(2)}) copy-start(bf16[8,4096]{1,0:T(8,128)(2,1)} %param.13) | copy-start | bytes 196612
Sparse Core Ops, SparseCore 0:
  41.8 41.2 all-reduce.1
  141.6 32.7 reduce-scatter.1
